TPU v7x, 32 devices: a whole 2x2x4 slice. The times are simulated.
32 devices in a mesh: grp: 2 (over y), band: 8 (over z, x), filt: 2 (over core).
Axes of the slice: x: 2, y: 2, z: 4, core: 2. Of those that a mesh axis runs over, the one named last changes fastest.
Arguments:
- coeff_maps: bfloat16 [128, 64, 512], P(('grp', 'filt'), 'band'), parts along dimension 0, may hold values from -0.75 to 0.75
- image: bfloat16 [6, 64, 512], P('grp', 'band'), parts along dimension 0, may hold values from -24 to 24
- target: bfloat16 [1024, 2, 3, 64, 64], P(('grp', 'band'), None, None, 'filt'), parts along dimension 0, may hold values from -1.5 to 1.5
- dual_rim: float32 [128, 768], P(('grp', 'filt')), parts along dimension 0, may hold values from -18 to 18, as said below
Outputs:
- dict_spectra: bfloat16 [1024, 2, 3, 64, 64], P(('grp', 'band'), None, None, 'filt'), parts along dimension 0
- dictionary: float32 [128, 768], P(('grp', 'filt')), parts along dimension 0
There are 2 independent parts, one for each index of `grp`. A program takes and returns all parts, laid end to end along the dimension named above; each array names one. Nothing has to cross between parts.
Inputs may be any that keep to these rules, and one draw needn't show every extreme that they name: `dual_rim`: a scaled dual variable on the filters' support.
All inputs are finite; a program needn't handle non-finite values.
Results may differ from a plain program's by a relative error of at most 0.0059.
Values may be sent and summed in bfloat16 or wider, within the bound.
No kernel may reach another device: no remote copies, remote signals or barrier semaphores. Data moves between devices by JAX's collectives and lax.ppermute only.
A program may use at most 128 MiB of HBM per device.

v0:
```python
import math
import jax
import jax.numpy as jnp
from jax import lax
from jax.sharding import PartitionSpec as P

K = 16
penalty = 1.0


def forward_columns(length):
    ramp = jnp.arange(length, dtype=jnp.int32)
    phases = ramp[:, None] * ramp[None, :] % length
    angles = phases.astype(jnp.float32) * (2.0 * math.pi / length)
    factor = 1.0 / math.sqrt(length)
    lookup = jnp.stack([jnp.cos(angles) * factor, -jnp.sin(angles) * factor], axis=2)
    return lookup.reshape(length, 2 * length).astype(jnp.bfloat16)


def forward_rows(length):
    ramp = jnp.arange(length, dtype=jnp.int32)
    phases = ramp[:, None] * ramp[None, :] % length
    angles = phases.astype(jnp.float32) * (2.0 * math.pi / length)
    factor = 1.0 / math.sqrt(length)
    return jnp.stack([jnp.cos(angles) * factor, jnp.sin(angles) * factor], axis=0).astype(
        jnp.bfloat16
    )


def inverse_rows(length, width):
    ramp = jnp.arange(length, dtype=jnp.int32)
    reach = jnp.arange(width, dtype=jnp.int32)
    phases = ramp[:, None] * reach[None, :] % length
    angles = phases.astype(jnp.float32) * (2.0 * math.pi / length)
    factor = 1.0 / math.sqrt(length)
    return jnp.stack([jnp.cos(angles) * factor, jnp.sin(angles) * factor], axis=1)


def inverse_columns(length, total_cols, width):
    freqs = jnp.arange(length, dtype=jnp.int32)
    reach = jnp.arange(width, dtype=jnp.int32)
    phases = freqs[:, None] * reach[None, :] % total_cols
    angles = phases.astype(jnp.float32) * (2.0 * math.pi / total_cols)
    factor = 1.0 / math.sqrt(total_cols)
    return jnp.stack([jnp.cos(angles) * factor, jnp.sin(angles) * factor], axis=1)


def spectra(slab_rows, lookup, freqs, members):
    height = slab_rows.shape[0]
    products = jnp.einsum("hk,tgh->ktg", slab_rows, lookup, preferred_element_type=jnp.float32)
    products = products.reshape(freqs, 2, members, 2, height)
    real_part = products[:, 0, :, 0] + products[:, 1, :, 1]
    imag_part = products[:, 1, :, 0] - products[:, 0, :, 1]
    return (real_part, imag_part)


def body(coeff_maps, image, target, dual_rim):
    filters, band_rows, width_cols = coeff_maps.shape
    channels = image.shape[0]
    band_count = lax.axis_size("band")
    height = band_rows * band_count
    per_band = width_cols // band_count
    col_lookup = forward_columns(width_cols)
    row_lookup = forward_rows(height)
    col_maps = jnp.einsum("mrn,nk->rkm", coeff_maps, col_lookup, preferred_element_type=jnp.float32)
    col_maps = col_maps.astype(jnp.bfloat16).reshape(band_rows, 2 * width_cols * filters)
    col_image = jnp.einsum("crn,nk->rkc", image, col_lookup, preferred_element_type=jnp.float32)
    col_image = col_image.astype(jnp.bfloat16).reshape(band_rows, 2 * width_cols * channels)
    got_maps, got_image = (
        lax.all_to_all(col_maps, "band", split_axis=1, concat_axis=0, tiled=True),
        lax.all_to_all(col_image, "band", split_axis=1, concat_axis=0, tiled=True),
    )
    x_re, x_im = spectra(got_maps, row_lookup, per_band, filters)
    s_re, s_im = spectra(got_image, row_lookup, per_band, channels)
    v_full = target.astype(jnp.float32)
    v_re = v_full[:, 0]
    v_im = v_full[:, 1]
    energy = jnp.sum(x_re * x_re + x_im * x_im, axis=1)
    cross_re = jnp.sum(x_re[:, None] * v_re - x_im[:, None] * v_im, axis=2)
    cross_im = jnp.sum(x_re[:, None] * v_im + x_im[:, None] * v_re, axis=2)
    energy, cross_re, cross_im = (
        lax.psum(energy.astype(jnp.bfloat16), "filt").astype(jnp.float32),
        lax.psum(cross_re.astype(jnp.bfloat16), "filt").astype(jnp.float32),
        lax.psum(cross_im.astype(jnp.bfloat16), "filt").astype(jnp.float32),
    )
    denom = penalty + energy[:, None, :]
    coef_re = (s_re - cross_re) / denom
    coef_im = (s_im - cross_im) / denom
    dict_real = v_re + x_re[:, None] * coef_re[:, :, None] + x_im[:, None] * coef_im[:, :, None]
    dict_imag = v_im + x_re[:, None] * coef_im[:, :, None] - x_im[:, None] * coef_re[:, :, None]
    dict_full = jnp.stack([dict_real, dict_imag], axis=1)
    dict_spectra = dict_full.astype(jnp.bfloat16)
    rim_lookup = inverse_rows(height, K)
    folded = jnp.einsum("qpcmg,gty->qpcmty", dict_full, rim_lookup, precision=lax.Precision.HIGHEST)
    rim_real = folded[:, 0, :, :, 0] - folded[:, 1, :, :, 1]
    rim_imag = folded[:, 0, :, :, 1] + folded[:, 1, :, :, 0]
    start_sum = jnp.zeros((filters, channels, K, K), jnp.float32)
    running = start_sum
    pieces = (
        lax.all_gather(rim_real.astype(jnp.bfloat16), "band", axis=0, tiled=True).astype(
            jnp.float32
        ),
        lax.all_gather(rim_imag.astype(jnp.bfloat16), "band", axis=0, tiled=True).astype(
            jnp.float32
        ),
    )
    length = pieces[0].shape[0]
    lookup = inverse_columns(length, width_cols, K)
    running = running + jnp.einsum(
        "qcmy,qx->mcyx", pieces[0], lookup[:, 0], precision=lax.Precision.HIGHEST
    )
    spatial = running - jnp.einsum(
        "qcmy,qx->mcyx", pieces[1], lookup[:, 1], precision=lax.Precision.HIGHEST
    )
    joined = spatial.reshape(filters, channels * K * K) + dual_rim
    spread = jnp.sqrt(jnp.mean(joined * joined, axis=1, keepdims=True))
    dictionary = joined / jnp.maximum(spread, 1.0)
    return (dict_spectra, dictionary)


def solution(mesh):
    placed = (
        P(("grp", "filt"), "band", None),
        P("grp", "band", None),
        P(("grp", "band"), None, None, "filt", None),
        P(("grp", "filt"), None),
    )
    return jax.shard_map(
        body,
        mesh=mesh,
        in_specs=placed,
        out_specs=(P(("grp", "band"), None, None, "filt", None), P(("grp", "filt"), None)),
        check_vma=False,
    )
```

profile of v0, /device:TPU:0, one launch (start us, length us, event | category | flops | bytes accessed | tf_op | source)
XLA Modules:
  0.0 297.8 jit_solution(11534772521772797656)
XLA Ops:
  7.2 4.4 %multiply_convert_fusion = (bf16[512,512,1]{1,0,2:T(8,128)(2,1)S(1)}, bf16[512,512,1]{1,0,2:T(8,128)(2,1)S(1)}) fusion(), kind=kLoop, calls=%fused_computation.42 | loop fusion | flops 4980736 | bytes 1048576 | tf_op jit(solution)/shard_map/convert.3
  11.6 0.1 pad_maximum_fusion.2
  11.7 1.0 copy.59
  12.7 0.4 convert_element_type.110
  13.1 0.4 fusion.15
  13.5 0.7 copy.69
  14.2 0.6 all_to_all.32
  14.9 0.9 copy.70
  15.7 7.3 %all-to-all-start.1 = ((bf16[8,8,384]{2,0,1:T(8,128)(2,1)}), bf16[8,8,384]{2,0,1:T(8,128)(2,1)S(1)}, u32[]{:S(2)}, u32[]{:S(2)}) async-start(bf16[8,8,384]{2,0,1:T(8,128)(2,1)} %copy.70), calls=%async_computation.1 | async-start | bytes 98304 | tf_op jit(solution)/shard_map/all_to_all | solution.py:71
  23.0 0.5 fusion.11
  23.5 1.0 copy.62
  24.5 2.3 all_to_all.28
  26.8 1.1 copy.63
  27.9 1.9 all-to-all-done.1
  29.8 4.1 %all-to-all-start = ((bf16[8,8,4096]{2,0,1:T(8,128)(2,1)}), bf16[8,8,4096]{2,0,1:T(8,128)(2,1)S(1)}, u32[]{:S(2)}, u32[]{:S(2)}) async-start(bf16[8,8,4096]{2,0,1:T(8,128)(2,1)} %copy.63), calls=%async_computation | async-start | bytes 1048576 | tf_op jit(solution)/shard_map/all_to_all | solution.py:70
  33.9 0.0 all-gather.7.cloned.1.call-start
  33.9 0.1 sine_multiply_fusion
  34.0 0.2 multiply_convert_fusion.2
  34.1 6.4 %copy_convert_fusion = f32[64,2,3,32,64]{4,0,3,2,1:T(8,128)} fusion(bf16[64,2,3,32,64]{4,3,2,1,0:T(8,128)(2,1)} %param.6), kind=kLoop, calls=%fused_computation.12 | loop fusion | flops 786432 | bytes 4718592 | tf_op jit(solution)/shard_map/convert_element_type | solution.py:75
  40.5 0.1 copy.71
  40.6 0.1 dot_general.35
  40.7 0.2 fusion.39
  40.9 6.9 %all-to-all-done = bf16[8,8,4096]{2,0,1:T(8,128)(2,1)S(1)} async-done(((bf16[8,8,4096]{2,0,1:T(8,128)(2,1)}), bf16[8,8,4096]{2,0,1:T(8,128)(2,1)S(1)}, u32[]{:S(2)}, u32[]{:S(2)}) %all-to-all-start) | async-done | bytes 524320 | tf_op jit(solution)/shard_map/all_to_all | solution.py:70
  47.9 0.5 copy.64
  48.4 0.9 fusion.22
  49.2 0.7 add_reduce_fusion
  49.9 0.6 slice-done
  50.5 1.4 slice-done.1
  51.9 1.1 fusion.4
  53.0 3.9 %all-reduce = (bf16[64,3,64]{2,0,1:T(8,128)(2,1)S(1)}, bf16[64,64]{1,0:T(8,128)(2,1)S(1)}, bf16[64,3,64]{2,0,1:T(8,128)(2,1)S(1)}) all-reduce(bf16[64,3,64]{2,0,1:T(8,128)(2,1)S(1)} %get-tuple-element.11, bf16[64,64]{1,0:T(8,128)(2,1)S(1)} %get-tuple-element.17, ...), channel_id=1, replica_groups=mesh['grp'=2,'band'=8,'filt'=2] {'filt'}, use_global_device_ids=true, to_apply=%region_5.6 | all-reduce | flops 28672 | bytes 114688 | tf_op jit(solution)/shard_map/psum | solution.py:84
  57.0 4.5 %multiply_add_fusion = (f32[64,1,3,32,64]{4,0,3,2,1:T(8,128)S(1)}, f32[64,1,3,32,64]{4,0,3,2,1:T(8,128)S(1)}) fusion(f32[64,2,3,32,64]{4,0,3,2,1:T(8,128)} %copy_convert_fusion, f32[64,3,64]{2,0,1:T(8,128)S(1)} %get-tuple-element.25, f32[64,32,64]{2,0,1:T(8,128)} %copy-done.3, f32[64,3,64]{2,0,1:T(8,128)S(1)} %get-tuple-element.24, f32[64,32,64]{2,0,1:T(8,128)} %copy-done.2), kind=kLoop, calls=%fused_computation.14 | loop fusion | flops 3145728 | bytes 7438336 | tf_op jit(solution)/shard_map/add | solution.py:89
  61.5 17.3 %fusion = f32[64,2,3,32,2,16]{0,5,4,3,2,1:T(8,128)S(1)} fusion(f32[64,1,3,32,64]{4,0,3,2,1:T(8,128)S(1)} %get-tuple-element.21, f32[64,1,3,32,64]{4,0,3,2,1:T(8,128)S(1)} %get-tuple-element.20, f32[64,1,16]{0,2,1:T(8,128)S(1)} %get-tuple-element.30, f32[64,1,16]{0,2,1:T(8,128)S(1)} %get-tuple-element.31), kind=kOutput, calls=%fused_computation.1 | convolution fusion | flops 302778368 | bytes 4726784 | tf_op jit(solution)/shard_map/qpcmg,gty->qpcmty/dot_general | solution.py:94
  78.9 1.1 fusion.30
  80.0 2.7 copy.77
  82.7 0.0 all-gather.7.cloned.1.call-update
  82.7 0.3 all-gather.5.cloned.1.call-start
  83.0 2.7 copy.75
  85.7 2.4 fusion.2
  88.1 3.7 %copy.80 = bf16[64,2,3,32,64]{4,3,2,1,0:T(8,128)(2,1)} copy(bf16[64,2,3,32,64]{4,0,3,2,1:T(8,128)(2,1)S(1)} %fusion.2) | data formatting | bytes 3145728
  91.7 89.3 %all-gather.7.cloned.1.call-done = bf16[512,1,3,32,1,16]{3,5,4,2,1,0:T(8,128)(2,1)} async-done(((bf16[64,1,3,32,1,16]{3,5,4,2,1,0:T(8,128)(2,1)}), bf16[512,1,3,32,1,16]{3,5,4,2,1,0:T(8,128)(2,1)}) %all-gather.7.cloned.1.call-update) | async-done | bytes 1572880 | tf_op jit(solution)/shard_map/all_gather | solution.py:103
  181.0 6.4 %copy.78 = bf16[512,1,3,32,1,16]{0,3,5,2,4,1:T(8,128)(2,1)S(1)} copy(bf16[512,1,3,32,1,16]{3,5,4,2,1,0:T(8,128)(2,1)} %all-gather.7.cloned.1.call-done) | data formatting | bytes 3145728 | tf_op jit(solution)/shard_map/all_gather | solution.py:103
  187.4 3.2 %fusion.7 = f32[16,3,32,16]{2,0,3,1:T(8,128)S(1)} fusion(bf16[512,1,3,32,1,16]{0,3,5,2,4,1:T(8,128)(2,1)S(1)} %copy.78), kind=kOutput, calls=%fused_computation.15 | convolution fusion | flops 151117824 | bytes 1671168 | tf_op jit(solution)/shard_map/qcmy,qx->mcyx/dot_general | solution.py:112
  190.5 89.9 %all-gather.5.cloned.1.call-done = bf16[512,1,3,32,1,16]{3,5,4,2,1,0:T(8,128)(2,1)} async-done(((bf16[64,1,3,32,1,16]{3,5,4,2,1,0:T(8,128)(2,1)}), bf16[512,1,3,32,1,16]{3,5,4,2,1,0:T(8,128)(2,1)}) %all-gather.5.cloned.1.call-update) | async-done | bytes 1572880 | tf_op jit(solution)/shard_map/all_gather | solution.py:100
  280.4 6.4 %copy.76 = bf16[512,1,3,32,1,16]{0,3,5,2,4,1:T(8,128)(2,1)S(1)} copy(bf16[512,1,3,32,1,16]{3,5,4,2,1,0:T(8,128)(2,1)} %all-gather.5.cloned.1.call-done) | data formatting | bytes 3145728 | tf_op jit(solution)/shard_map/all_gather | solution.py:100
  286.8 3.2 %fusion.12 = f32[16,3,32,16]{2,0,3,1:T(8,128)S(1)} fusion(f32[16,3,32,16]{2,0,3,1:T(8,128)S(1)} %fusion.7, bf16[512,1,3,32,1,16]{0,3,5,2,4,1:T(8,128)(2,1)S(1)} %copy.76), kind=kOutput, calls=%fused_computation.24 | convolution fusion | flops 151142400 | bytes 1769472 | tf_op jit(solution)/shard_map/qcmy,qx->mcyx/dot_general | solution.py:109
  290.0 0.2 copy.79
  290.1 0.1 multiply_reduce_fusion
  290.3 0.7 broadcast_divide_fusion
  (19 shorter events, 0.1 us)
Async XLA Ops:
  7.2 15.8 %copy-start = (bf16[32,8,512]{2,1,0:T(8,128)(2,1)S(1)}, bf16[32,8,512]{2,1,0:T(8,128)(2,1)}, u32[]{:S(2)}) copy-start(bf16[32,8,512]{2,1,0:T(8,128)(2,1)} %param.4) | copy-start | bytes 786436
  11.6 1.6 copy-start.5
  15.7 14.0 %all-to-all-start.1 = ((bf16[8,8,384]{2,0,1:T(8,128)(2,1)}), bf16[8,8,384]{2,0,1:T(8,128)(2,1)S(1)}, u32[]{:S(2)}, u32[]{:S(2)}) async-start(bf16[8,8,384]{2,0,1:T(8,128)(2,1)} %copy.70), calls=%async_computation.1 | async-start | bytes 98304 | tf_op jit(solution)/shard_map/all_to_all | solution.py:71
  29.8 18.1 %all-to-all-start = ((bf16[8,8,4096]{2,0,1:T(8,128)(2,1)}), bf16[8,8,4096]{2,0,1:T(8,128)(2,1)S(1)}, u32[]{:S(2)}, u32[]{:S(2)}) async-start(bf16[8,8,4096]{2,0,1:T(8,128)(2,1)} %copy.63), calls=%async_computation | async-start | bytes 1048576 | tf_op jit(solution)/shard_map/all_to_all | solution.py:70
  33.9 147.1 %all-gather.7.cloned.1.call-start = ((), (), s32[]{:S(2)}) async-start(), calls=%async_computation.3 | async-start | bytes 7077888 | tf_op jit(solution)/shard_map/all_gather | solution.py:103
  48.3 2.2 slice-start
  48.3 3.6 %slice-start.1 = ((s8[6291456]{0:T(1024)(128)(4,1)}), s8[2097152]{0:T(1024)(128)(4,1)S(1)}, s32[]{:S(2)}) async-start(s8[6291456]{0:T(1024)(128)(4,1)} %bitcast.128), calls=%async_computation.5 | async-start | bytes 4194304
  49.9 3.1 %copy-start.2 = (f32[64,32,64]{2,0,1:T(8,128)}, f32[64,32,64]{2,0,1:T(8,128)S(1)}, u32[]{:S(2)}) copy-start(f32[64,32,64]{2,0,1:T(8,128)S(1)} %get-tuple-element.18) | copy-start | bytes 1572868
  49.9 3.1 %copy-start.3 = (f32[64,32,64]{2,0,1:T(8,128)}, f32[64,32,64]{2,0,1:T(8,128)S(1)}, u32[]{:S(2)}) copy-start(f32[64,32,64]{2,0,1:T(8,128)S(1)} %get-tuple-element.19) | copy-start | bytes 1572868
  61.5 17.4 %copy-start.1 = (f32[64,1,3,32,64]{4,0,3,2,1:T(8,128)}, f32[64,1,3,32,64]{4,0,3,2,1:T(8,128)S(1)}, u32[]{:S(2)}) copy-start(f32[64,1,3,32,64]{4,0,3,2,1:T(8,128)S(1)} %get-tuple-element.21) | copy-start | bytes 4718596
  82.7 197.7 %all-gather.5.cloned.1.call-start = ((), (), s32[]{:S(2)}) async-start(), calls=%async_computation.2 | async-start | bytes 7077888 | tf_op jit(solution)/shard_map/all_gather | solution.py:100
  190.5 99.6 %copy-start.4 = (f32[32,768]{1,0:T(8,128)S(1)}, f32[32,768]{1,0:T(8,128)}, u32[]{:S(2)}) copy-start(f32[32,768]{1,0:T(8,128)} %param.7) | copy-start | bytes 294916
Sparse Core Ops, SparseCore 0:
  82.9 98.1 all-gather.6
  183.2 97.1 all-gather.4
where the time goes:
time: 298 us
  waiting for transfers between devices  188 us (63%)
  local copies, waits for them, and re-layouts  32.7 us (11%)
  matrix products  25.6 us (9%)
  other arithmetic  21.7 us (7%)
  between operations  14.3 us (5%)
  starting transfers between devices  11.6 us (4%)
  blocking collectives  3.9 us (1%)
    all_gather x1, waiting for transfers between devices, body(): lax.all_gather(rim_real.astype(jnp.bfloat16), 'band', axis=0, tiled=True)  89.9 us
    all_gather x1, waiting for transfers between devices, body(): lax.all_gather(rim_imag.astype(jnp.bfloat16), 'band', axis=0, tiled=True)  89.3 us
    dot_general x1, matrix products, body(): jnp.einsum('qpcmg,gty->qpcmty', dict_full, rim_lookup, precision=lax.Prec...  17.3 us
    all_to_all x1, starting transfers between devices, body(): lax.all_to_all(col_image, 'band', split_axis=1, concat_axis=0, tiled=True)  7.25 us
    all_to_all x1, waiting for transfers between devices, body(): lax.all_to_all(col_maps, 'band', split_axis=1, concat_axis=0, tiled=True)  6.91 us
    convert_element_type x1, other arithmetic, body(): v_full = target.astype(jnp.float32)  6.37 us
    all_gather x1, local copies, waits for them, and re-layouts, body(): lax.all_gather(rim_imag.astype(jnp.bfloat16), 'band', axis=0, tiled=True)  6.36 us
    all_gather x1, local copies, waits for them, and re-layouts, body(): lax.all_gather(rim_real.astype(jnp.bfloat16), 'band', axis=0, tiled=True)  6.36 us
  transfers between devices with their start and end apart: 4, of which 4 were waited for; matrix products, arithmetic and copies ran while one was open for 9% of the time, Pallas kernels for 0%

commit v1 on v0

--- a/solution.py
+++ b/solution.py
@@ -6,6 +6,18 @@
 
 K = 16
 penalty = 1.0
+
+
+def collect(x, axis, dim):
+    ways, here = (lax.axis_size(axis), lax.axis_index(axis))
+    grown, reach = (x, 1)
+    while reach < ways:
+        theirs = lax.ppermute(grown, axis, [(d, d ^ reach) for d in range(ways)])
+        mine_first = jnp.concatenate([grown, theirs], axis=dim)
+        theirs_first = jnp.concatenate([theirs, grown], axis=dim)
+        grown = jnp.where(here & reach == 0, mine_first, theirs_first)
+        reach = 2 * reach
+    return grown
 
 
 def forward_columns(length):
@@ -100,9 +112,7 @@
         lax.all_gather(rim_real.astype(jnp.bfloat16), "band", axis=0, tiled=True).astype(
             jnp.float32
         ),
-        lax.all_gather(rim_imag.astype(jnp.bfloat16), "band", axis=0, tiled=True).astype(
-            jnp.float32
-        ),
+        collect(rim_imag.astype(jnp.bfloat16), "band", 0).astype(jnp.float32),
     )
     length = pieces[0].shape[0]
     lookup = inverse_columns(length, width_cols, K)

time: 298 us -> 238 us (0.80)
  waiting for transfers between devices: 188 us -> 127 us
  local copies, waits for them, and re-layouts: 32.7 us -> 23.6 us
  other arithmetic: 21.7 us -> 29.5 us
    ppermute x0 -> x3, waiting for transfers between devices: none -> 112 us  [collect(): theirs = lax.ppermute(grown, axis, [(d, d ^ reach) for d in range(ways)])]
    all_gather x1 -> x0, waiting for transfers between devices: 89.3 us -> none  [body(): lax.all_gather(rim_imag.astype(jnp.bfloat16), 'band', axis=0, tiled=True)]
    all_gather x1, waiting for transfers between devices: 89.9 us -> 6.2 us  [body(): lax.all_gather(rim_real.astype(jnp.bfloat16), 'band', axis=0, tiled=True)]
    select_n x0 -> x3, other arithmetic: none -> 7.67 us  [collect(): grown = jnp.where(here & reach == 0, mine_first, theirs_first)]
    all_gather x1 -> x0, local copies, waits for them, and re-layouts: 6.36 us -> none  [body(): lax.all_gather(rim_imag.astype(jnp.bfloat16), 'band', axis=0, tiled=True)]
  transfers between devices with their start and end apart: 4 -> 6, of which waited for: 4 -> 6; matrix products, arithmetic and copies ran while one was open for 9% -> 10% of each run, Pallas kernels for 0% -> 0%
where the time goes in v1:
time: 238 us; the launch traced here: 237 us
  waiting for transfers between devices  127 us (53%)
  other arithmetic  29.5 us (12%)
  matrix products  25.8 us (11%)
  local copies, waits for them, and re-layouts  23.6 us (10%)
  between operations  14.3 us (6%)
  starting transfers between devices  12.9 us (5%)
  blocking collectives  3.9 us (2%)
    ppermute x3, waiting for transfers between devices, collect(): theirs = lax.ppermute(grown, axis, [(d, d ^ reach) for d in range(ways)])  112 us
    dot_general x1, matrix products, body(): jnp.einsum('qpcmg,gty->qpcmty', dict_full, rim_lookup, precision=lax.Prec...  17.3 us
    select_n x3, other arithmetic, collect(): grown = jnp.where(here & reach == 0, mine_first, theirs_first)  7.67 us
    all_to_all x1, starting transfers between devices, body(): lax.all_to_all(col_image, 'band', split_axis=1, concat_axis=0, tiled=True)  7.25 us
    all_to_all x1, waiting for transfers between devices, body(): lax.all_to_all(col_maps, 'band', split_axis=1, concat_axis=0, tiled=True)  6.91 us
    convert_element_type x1, other arithmetic, body(): v_full = target.astype(jnp.float32)  6.37 us
    all_gather x1, local copies, waits for them, and re-layouts, body(): lax.all_gather(rim_real.astype(jnp.bfloat16), 'band', axis=0, tiled=True)  6.36 us
    all_gather x1, waiting for transfers between devices, body(): lax.all_gather(rim_real.astype(jnp.bfloat16), 'band', axis=0, tiled=True)  6.2 us
  transfers between devices with their start and end apart: 6, of which 6 were waited for; matrix products, arithmetic and copies ran while one was open for 10% of the time, Pallas kernels for 0%

profile of v1, /device:TPU:0, one launch (start us, length us, event | category | flops | bytes accessed | tf_op | source)
XLA Modules:
  0.0 237.4 jit_solution(510654567191855901)
XLA Ops:
  7.2 4.4 %multiply_convert_fusion = (bf16[512,512,1]{1,0,2:T(8,128)(2,1)S(1)}, bf16[512,512,1]{1,0,2:T(8,128)(2,1)S(1)}) fusion(), kind=kLoop, calls=%fused_computation.43 | loop fusion | flops 4980736 | bytes 1048576 | tf_op jit(solution)/shard_map/convert.3
  11.6 0.1 pad_maximum_fusion.2
  11.7 1.0 copy.58
  12.7 0.4 convert_element_type.110
  13.1 0.4 fusion.15
  13.5 0.7 copy.68
  14.2 0.6 all_to_all.32
  14.9 0.9 copy.69
  15.7 7.3 %all-to-all-start.1 = ((bf16[8,8,384]{2,0,1:T(8,128)(2,1)}), bf16[8,8,384]{2,0,1:T(8,128)(2,1)S(1)}, u32[]{:S(2)}, u32[]{:S(2)}) async-start(bf16[8,8,384]{2,0,1:T(8,128)(2,1)} %copy.69), calls=%async_computation.1 | async-start | bytes 98304 | tf_op jit(solution)/shard_map/all_to_all | solution.py:83
  23.0 0.5 fusion.11
  23.5 1.0 copy.61
  24.5 2.3 all_to_all.28
  26.8 1.1 copy.62
  27.9 1.9 all-to-all-done.1
  29.8 4.1 %all-to-all-start = ((bf16[8,8,4096]{2,0,1:T(8,128)(2,1)}), bf16[8,8,4096]{2,0,1:T(8,128)(2,1)S(1)}, u32[]{:S(2)}, u32[]{:S(2)}) async-start(bf16[8,8,4096]{2,0,1:T(8,128)(2,1)} %copy.62), calls=%async_computation | async-start | bytes 1048576 | tf_op jit(solution)/shard_map/all_to_all | solution.py:82
  34.0 0.2 multiply_convert_fusion.2
  34.1 6.4 %copy_convert_fusion = f32[64,2,3,32,64]{4,0,3,2,1:T(8,128)} fusion(bf16[64,2,3,32,64]{4,3,2,1,0:T(8,128)(2,1)} %param.6), kind=kLoop, calls=%fused_computation.12 | loop fusion | flops 786432 | bytes 4718592 | tf_op jit(solution)/shard_map/convert_element_type | solution.py:87
  40.5 0.1 copy.70
  40.6 0.1 dot_general.35
  40.7 0.2 fusion.40
  40.9 6.9 %all-to-all-done = bf16[8,8,4096]{2,0,1:T(8,128)(2,1)S(1)} async-done(((bf16[8,8,4096]{2,0,1:T(8,128)(2,1)}), bf16[8,8,4096]{2,0,1:T(8,128)(2,1)S(1)}, u32[]{:S(2)}, u32[]{:S(2)}) %all-to-all-start) | async-done | bytes 524320 | tf_op jit(solution)/shard_map/all_to_all | solution.py:82
  47.9 0.5 copy.63
  48.4 0.9 fusion.22
  49.2 0.7 add_reduce_fusion
  49.9 0.6 slice-done
  50.5 1.4 slice-done.1
  51.9 1.1 fusion.4
  53.0 3.9 %all-reduce = (bf16[64,3,64]{2,0,1:T(8,128)(2,1)S(1)}, bf16[64,64]{1,0:T(8,128)(2,1)S(1)}, bf16[64,3,64]{2,0,1:T(8,128)(2,1)S(1)}) all-reduce(bf16[64,3,64]{2,0,1:T(8,128)(2,1)S(1)} %get-tuple-element.11, bf16[64,64]{1,0:T(8,128)(2,1)S(1)} %get-tuple-element.17, ...), channel_id=1, replica_groups=mesh['grp'=2,'band'=8,'filt'=2] {'filt'}, use_global_device_ids=true, to_apply=%region_5.6 | all-reduce | flops 28672 | bytes 114688 | tf_op jit(solution)/shard_map/psum | solution.py:96
  57.0 4.5 %multiply_add_fusion = (f32[64,1,3,32,64]{4,0,3,2,1:T(8,128)S(1)}, f32[64,1,3,32,64]{4,0,3,2,1:T(8,128)S(1)}) fusion(f32[64,2,3,32,64]{4,0,3,2,1:T(8,128)} %copy_convert_fusion, f32[64,3,64]{2,0,1:T(8,128)S(1)} %get-tuple-element.25, f32[64,32,64]{2,0,1:T(8,128)} %copy-done.3, f32[64,3,64]{2,0,1:T(8,128)S(1)} %get-tuple-element.24, f32[64,32,64]{2,0,1:T(8,128)} %copy-done.2), kind=kLoop, calls=%fused_computation.14 | loop fusion | flops 3145728 | bytes 7438336 | tf_op jit(solution)/shard_map/add | solution.py:101
  61.5 17.3 %fusion = f32[64,2,3,32,2,16]{0,5,4,3,2,1:T(8,128)S(1)} fusion(f32[64,1,3,32,64]{4,0,3,2,1:T(8,128)S(1)} %get-tuple-element.21, f32[64,1,3,32,64]{4,0,3,2,1:T(8,128)S(1)} %get-tuple-element.20, f32[64,1,16]{0,2,1:T(8,128)S(1)} %get-tuple-element.30, f32[64,1,16]{0,2,1:T(8,128)S(1)} %get-tuple-element.31), kind=kOutput, calls=%fused_computation.1 | convolution fusion | flops 302778368 | bytes 4726784 | tf_op jit(solution)/shard_map/qpcmg,gty->qpcmty/dot_general | solution.py:106
  78.9 1.1 fusion.31
  79.9 2.7 %copy.74 = bf16[64,1,3,32,1,16]{3,5,4,2,1,0:T(8,128)(2,1)} copy(bf16[64,1,3,32,1,16]{0,5,4,3,2,1:T(8,128)(2,1)} %get-tuple-element.23) | data formatting | bytes 393216 | tf_op jit(solution)/shard_map/convert_element_type | solution.py:112
  82.6 1.5 collective-permute-start
  84.1 12.2 %collective-permute-done = bf16[64,3,32,16]{0,3,2,1:T(8,128)(2,1)} collective-permute-done((bf16[64,3,32,16]{0,3,2,1:T(8,128)(2,1)}, bf16[64,3,32,16]{0,3,2,1:T(8,128)(2,1)}, u32[]{:S(2)}, u32[]{:S(2)}) %collective-permute-start) | collective-permute-done | bytes 196640 | tf_op jit(solution)/shard_map/ppermute | solution.py:15
  96.4 2.6 %maximum_select_fusion.2 = bf16[128,3,32,16]{0,3,2,1:T(8,128)(2,1)} fusion(bf16[64,3,32,16]{0,3,2,1:T(8,128)(2,1)} %collective-permute-done, bf16[64,3,32,16]{0,3,2,1:T(8,128)(2,1)} %get-tuple-element.22, pred[]{:T(512)S(6)} %eq.19), kind=kLoop, calls=%fused_computation.54 | loop fusion | flops 1769472 | bytes 786433 | tf_op jit(solution)/shard_map/jit(_where)/select_n | solution.py:18
  98.9 27.9 %collective-permute-done.1 = bf16[128,3,32,16]{0,3,2,1:T(8,128)(2,1)} collective-permute-done((bf16[128,3,32,16]{0,3,2,1:T(8,128)(2,1)}, bf16[128,3,32,16]{0,3,2,1:T(8,128)(2,1)}, u32[]{:S(2)}, u32[]{:S(2)}) %collective-permute-start.1) | collective-permute-done | bytes 393248 | tf_op jit(solution)/shard_map/ppermute | solution.py:15
  126.9 2.5 %maximum_select_fusion.1 = bf16[256,3,32,16]{0,3,2,1:T(8,128)(2,1)} fusion(bf16[128,3,32,16]{0,3,2,1:T(8,128)(2,1)} %collective-permute-done.1, bf16[128,3,32,16]{0,3,2,1:T(8,128)(2,1)} %maximum_select_fusion.2, pred[]{:T(512)S(6)} %eq.18), kind=kLoop, calls=%fused_computation.52 | loop fusion | flops 3538944 | bytes 1572865 | tf_op jit(solution)/shard_map/jit(_where)/select_n | solution.py:18
  129.4 2.6 %fusion.2 = bf16[64,2,3,32,64]{4,0,3,2,1:T(8,128)(2,1)S(1)} fusion(f32[64,1,3,32,64]{4,0,3,2,1:T(8,128)} %copy-done.1, f32[64,1,3,32,64]{4,0,3,2,1:T(8,128)S(1)} %get-tuple-element.20), kind=kLoop, calls=%fused_computation.3 | loop fusion | flops 786432 | bytes 4718592 | tf_op jit(solution)/shard_map/convert_element_type | solution.py:104
  132.0 3.7 %copy.78 = bf16[64,2,3,32,64]{4,3,2,1,0:T(8,128)(2,1)} copy(bf16[64,2,3,32,64]{4,0,3,2,1:T(8,128)(2,1)S(1)} %fusion.2) | data formatting | bytes 3145728
  135.7 72.2 %collective-permute-done.2 = bf16[256,3,32,16]{0,3,2,1:T(8,128)(2,1)} collective-permute-done((bf16[256,3,32,16]{0,3,2,1:T(8,128)(2,1)}, bf16[256,3,32,16]{0,3,2,1:T(8,128)(2,1)}, u32[]{:S(2)}, u32[]{:S(2)}) %collective-permute-start.2) | collective-permute-done | bytes 786464 | tf_op jit(solution)/shard_map/ppermute | solution.py:15
  207.8 2.6 %maximum_select_fusion = bf16[512,3,32,16]{0,3,2,1:T(8,128)(2,1)S(1)} fusion(bf16[256,3,32,16]{0,3,2,1:T(8,128)(2,1)} %collective-permute-done.2, bf16[256,3,32,16]{0,3,2,1:T(8,128)(2,1)} %maximum_select_fusion.1, pred[]{:T(512)S(6)} %eq.17), kind=kLoop, calls=%fused_computation.15 | loop fusion | flops 7077888 | bytes 3145729 | tf_op jit(solution)/shard_map/jit(_where)/select_n | solution.py:18
  210.4 6.2 %all-gather.3.cloned.1.call-done = bf16[512,1,3,32,1,16]{3,5,4,2,1,0:T(8,128)(2,1)} async-done(((bf16[64,1,3,32,1,16]{3,5,4,2,1,0:T(8,128)(2,1)}), bf16[512,1,3,32,1,16]{3,5,4,2,1,0:T(8,128)(2,1)}) %all-gather.3.cloned.1.call-update) | async-done | bytes 1572880 | tf_op jit(solution)/shard_map/all_gather | solution.py:112
  216.6 6.4 %copy.75 = bf16[512,1,3,32,1,16]{0,3,5,2,4,1:T(8,128)(2,1)S(1)} copy(bf16[512,1,3,32,1,16]{3,5,4,2,1,0:T(8,128)(2,1)} %all-gather.3.cloned.1.call-done) | data formatting | bytes 3145728 | tf_op jit(solution)/shard_map/all_gather | solution.py:112
  223.0 3.2 %fusion.7 = f32[16,3,32,16]{2,0,3,1:T(8,128)S(1)} fusion(bf16[512,1,3,32,1,16]{0,3,5,2,4,1:T(8,128)(2,1)S(1)} %copy.75), kind=kOutput, calls=%fused_computation.16 | convolution fusion | flops 151117824 | bytes 1671168 | tf_op jit(solution)/shard_map/qcmy,qx->mcyx/dot_general | solution.py:119
  226.2 3.3 %fusion.12 = f32[16,3,32,16]{2,0,3,1:T(8,128)S(1)} fusion(f32[16,3,32,16]{2,0,3,1:T(8,128)S(1)} %fusion.7, bf16[512,3,32,16]{0,3,2,1:T(8,128)(2,1)S(1)} %maximum_select_fusion), kind=kOutput, calls=%fused_computation.25 | convolution fusion | flops 151142400 | bytes 1769472 | tf_op jit(solution)/shard_map/qcmy,qx->mcyx/dot_general | solution.py:122
  229.5 0.2 copy.77
  229.6 0.1 multiply_reduce_fusion
  229.8 0.7 broadcast_divide_fusion
  (23 shorter events, 0.2 us)
Async XLA Ops:
  7.2 15.8 %copy-start = (bf16[32,8,512]{2,1,0:T(8,128)(2,1)S(1)}, bf16[32,8,512]{2,1,0:T(8,128)(2,1)}, u32[]{:S(2)}) copy-start(bf16[32,8,512]{2,1,0:T(8,128)(2,1)} %param.4) | copy-start | bytes 786436
  11.6 1.6 copy-start.5
  15.7 14.0 %all-to-all-start.1 = ((bf16[8,8,384]{2,0,1:T(8,128)(2,1)}), bf16[8,8,384]{2,0,1:T(8,128)(2,1)S(1)}, u32[]{:S(2)}, u32[]{:S(2)}) async-start(bf16[8,8,384]{2,0,1:T(8,128)(2,1)} %copy.69), calls=%async_computation.1 | async-start | bytes 98304 | tf_op jit(solution)/shard_map/all_to_all | solution.py:83
  29.8 18.1 %all-to-all-start = ((bf16[8,8,4096]{2,0,1:T(8,128)(2,1)}), bf16[8,8,4096]{2,0,1:T(8,128)(2,1)S(1)}, u32[]{:S(2)}, u32[]{:S(2)}) async-start(bf16[8,8,4096]{2,0,1:T(8,128)(2,1)} %copy.62), calls=%async_computation | async-start | bytes 1048576 | tf_op jit(solution)/shard_map/all_to_all | solution.py:82
  33.9 182.8 %all-gather.3.cloned.1.call-start = ((), (), s32[]{:S(2)}) async-start(), calls=%async_computation.2 | async-start | bytes 7077888 | tf_op jit(solution)/shard_map/all_gather | solution.py:112
  48.3 2.2 slice-start
  48.3 3.6 %slice-start.1 = ((s8[6291456]{0:T(1024)(128)(4,1)}), s8[2097152]{0:T(1024)(128)(4,1)S(1)}, s32[]{:S(2)}) async-start(s8[6291456]{0:T(1024)(128)(4,1)} %bitcast.125), calls=%async_computation.4 | async-start | bytes 4194304
  49.9 3.1 %copy-start.2 = (f32[64,32,64]{2,0,1:T(8,128)}, f32[64,32,64]{2,0,1:T(8,128)S(1)}, u32[]{:S(2)}) copy-start(f32[64,32,64]{2,0,1:T(8,128)S(1)} %get-tuple-element.18) | copy-start | bytes 1572868
  49.9 3.1 %copy-start.3 = (f32[64,32,64]{2,0,1:T(8,128)}, f32[64,32,64]{2,0,1:T(8,128)S(1)}, u32[]{:S(2)}) copy-start(f32[64,32,64]{2,0,1:T(8,128)S(1)} %get-tuple-element.19) | copy-start | bytes 1572868
  61.5 17.4 %copy-start.1 = (f32[64,1,3,32,64]{4,0,3,2,1:T(8,128)}, f32[64,1,3,32,64]{4,0,3,2,1:T(8,128)S(1)}, u32[]{:S(2)}) copy-start(f32[64,1,3,32,64]{4,0,3,2,1:T(8,128)S(1)} %get-tuple-element.21) | copy-start | bytes 4718596
  82.6 13.7 %collective-permute-start = (bf16[64,3,32,16]{0,3,2,1:T(8,128)(2,1)}, bf16[64,3,32,16]{0,3,2,1:T(8,128)(2,1)}, u32[]{:S(2)}, u32[]{:S(2)}) collective-permute-start(bf16[64,3,32,16]{0,3,2,1:T(8,128)(2,1)} %get-tuple-element.22), channel_id=1, source_target_pairs={{0,2},{2,0},{4,6},{6,4},{8,10},{10,8},{12,14},{14,12},{1,3},{3,1},... | collective-permute-start | bytes 589832 | tf_op jit(solution)/shard_map/ppermute | solution.py:15
  98.9 27.9 %collective-permute-start.1 = (bf16[128,3,32,16]{0,3,2,1:T(8,128)(2,1)}, bf16[128,3,32,16]{0,3,2,1:T(8,128)(2,1)}, u32[]{:S(2)}, u32[]{:S(2)}) collective-permute-start(bf16[128,3,32,16]{0,3,2,1:T(8,128)(2,1)} %maximum_select_fusion.2), channel_id=1, source_target_pairs={{0,4},{2,6},{4,0},{6,2},{8,12},{10,14},{12,8},{14,10},{1,5},{3,7},... | collective-permute-start | bytes 1179656 | tf_op jit(solution)/shard_map/ppermute | solution.py:15
  129.4 78.5 %collective-permute-start.2 = (bf16[256,3,32,16]{0,3,2,1:T(8,128)(2,1)}, bf16[256,3,32,16]{0,3,2,1:T(8,128)(2,1)}, u32[]{:S(2)}, u32[]{:S(2)}) collective-permute-start(bf16[256,3,32,16]{0,3,2,1:T(8,128)(2,1)} %maximum_select_fusion.1), channel_id=1, source_target_pairs={{0,8},{2,10},{4,12},{6,14},{8,0},{10,2},{12,4},{14,6},{1,9},{3,11}... | collective-permute-start | bytes 2359304 | tf_op jit(solution)/shard_map/ppermute | solution.py:15
  223.0 6.6 %copy-start.4 = (f32[32,768]{1,0:T(8,128)S(1)}, f32[32,768]{1,0:T(8,128)}, u32[]{:S(2)}) copy-start(f32[32,768]{1,0:T(8,128)} %param.7) | copy-start | bytes 294916
Sparse Core Ops, SparseCore 0:
  82.8 133.8 all-gather.2
